TPU v7x, 32 devices: a whole 2x2x4 slice. The times are simulated.
32 devices in a mesh: query: 8 (over z, y), item: 4 (over x, core).
Axes of the slice: x: 2, y: 2, z: 4, core: 2. Of those that a mesh axis runs over, the one named last changes fastest.
Arguments:
- query_emb: bfloat16 [2048, 256], P(('query', 'item')), may hold values from -400 to 400
- targets: int32 [2048], P('query'), may hold values from 0 to 8191, as said below
- eligible_tiles: int32 [32, 32], P('query', 'item'), may hold values from 0 to 1, as said below
- item_feats: bfloat16 [4, 2048, 512], P('item', 'query'), may hold values from -6 to 6
- w_first: bfloat16 [512, 1024], replicated, may hold values from -0.25 to 0.25
- w_second: bfloat16 [1024, 256], replicated, may hold values from -0.1875 to 0.1875
Outputs:
- loss: float32 [2048], P(('query', 'item'))
- query_grad: float32 [2048, 256], P(('query', 'item'))
- w_first_grad: float32 [512, 1024], replicated
- w_second_grad: float32 [1024, 256], replicated
Inputs may be any that keep to these rules, and one draw needn't show every extreme that they name: `eligible_tiles`: every row has at least one 1. The block targets[q] // 256 is marked 1 in row q // 64 of eligible_tiles.
All inputs are finite; a program needn't handle non-finite values.
Results may differ from a plain program's by a relative error of at most 0.007.
Values may be sent and summed in bfloat16 or wider, within the bound.
A program may use at most 64 MiB of HBM per device.

v0:
```python
import math
import jax
import jax.numpy as jnp
from jax import lax
from jax.sharding import PartitionSpec as P

BOTH = ("query", "item")


def on_device(query_emb, targets, eligible_tiles, item_feats, w_first, w_second):
    q_rows = query_emb.shape[0]
    item_count = lax.axis_size("item")
    query_count = lax.axis_size("query")
    item_pos = lax.axis_index("item")
    query_pos = lax.axis_index("query")
    tokens = item_feats.reshape(item_feats.shape[1], item_feats.shape[2])
    block_rows = tokens.shape[0]
    queries = lax.all_gather(query_emb, "query", axis=0, tiled=True)
    own_targets = lax.dynamic_slice_in_dim(targets, item_pos * q_rows, q_rows, 0)
    small = jnp.concatenate([eligible_tiles.reshape(-1), own_targets])
    small = lax.all_gather(small, BOTH, axis=0).reshape(query_count, item_count, -1)
    flags = small[:, :, : eligible_tiles.size].reshape(
        (query_count, item_count) + eligible_tiles.shape
    )
    flags = lax.dynamic_slice(
        flags, (0, 0, item_pos, query_pos), (query_count, item_count, 1, 1)
    ).reshape(query_count, item_count)
    wanted = lax.dynamic_slice_in_dim(small[:, :, eligible_tiles.size :], item_pos, 1, 1).reshape(
        -1
    )
    pre_act = jnp.dot(tokens, w_first, preferred_element_type=jnp.float32)
    hidden = jax.nn.silu(pre_act).astype(jnp.bfloat16)
    own_emb = jnp.dot(hidden, w_second, preferred_element_type=jnp.float32).astype(jnp.bfloat16)
    items = lax.all_gather(own_emb, "item", axis=0, tiled=True)
    block_of = jnp.arange(item_count, dtype=jnp.int32) * query_count + query_pos
    item_ids = (
        block_of[:, None] * block_rows + jnp.arange(block_rows, dtype=jnp.int32)[None, :]
    ).reshape(-1)
    live = jnp.broadcast_to(
        flags[:, None, :, None] > 0, (query_count, q_rows, item_count, block_rows)
    ).reshape(query_count * q_rows, item_count * block_rows)
    scores = 0.25 * jnp.einsum("qe,ie->qi", queries, items, preferred_element_type=jnp.float32)
    hit = item_ids[None, :] == wanted[:, None]
    masked = jnp.where(live, scores, -1e30)
    top = jnp.max(masked, axis=1)
    total = jnp.sum(jnp.where(live, jnp.exp(masked - top[:, None]), 0.0), axis=1)
    positive = jnp.sum(jnp.where(hit, scores, 0.0), axis=1)
    stats = lax.all_gather(jnp.stack([top, total, positive]), "query", axis=0)
    all_top = jnp.max(stats[:, 0], axis=0)
    all_total = jnp.sum(stats[:, 1] * jnp.exp(stats[:, 0] - all_top[None]), axis=0)
    log_norm = all_top + jnp.log(all_total)
    loss = lax.dynamic_slice_in_dim(
        log_norm - jnp.sum(stats[:, 2], axis=0), query_pos * q_rows, q_rows, 0
    )
    weights = jnp.where(live, jnp.exp(masked - log_norm[:, None]), 0.0)
    coeffs = (weights - hit.astype(jnp.float32)).astype(jnp.bfloat16)
    e_part = 0.25 * jnp.einsum("qi,qe->ie", coeffs, queries, preferred_element_type=jnp.float32)
    own_grad = lax.psum_scatter(e_part, "item", scatter_dimension=0, tiled=True).astype(
        jnp.bfloat16
    )
    q_part = 0.25 * jnp.dot(coeffs, items, preferred_element_type=jnp.float32)
    query_grad = lax.psum_scatter(q_part, "query", scatter_dimension=0, tiled=True)
    second_term = jnp.einsum("ih,ie->he", hidden, own_grad, preferred_element_type=jnp.float32)
    hid_grad = jnp.einsum("ie,he->ih", own_grad, w_second, preferred_element_type=jnp.float32)
    gate_sig = jax.nn.sigmoid(pre_act)
    pre_grad = (hid_grad * gate_sig * (1.0 + pre_act * (1.0 - gate_sig))).astype(jnp.bfloat16)
    first_term = jnp.einsum("id,ih->dh", tokens, pre_grad, preferred_element_type=jnp.float32)
    tower_sums = lax.psum((first_term, second_term), BOTH)
    grad_scale = 1.0 / math.sqrt(block_rows * query_count * item_count)
    return (loss, query_grad, tower_sums[0] * grad_scale, tower_sums[1] * grad_scale)


def solution(mesh):
    return jax.shard_map(
        on_device,
        mesh=mesh,
        in_specs=(
            P(("query", "item"), None),
            P("query"),
            P("query", "item"),
            P("item", "query", None),
            P(),
            P(),
        ),
        out_specs=(P(("query", "item")), P(("query", "item"), None), P(), P()),
        check_vma=False,
    )
```

profile of v0, /device:TPU:0, one launch (start us, length us, event | category | flops | bytes accessed | tf_op | source)
XLA Modules:
  0.0 311.0 jit_solution(3521980565822129825)
XLA Ops:
  8.0 0.0 copy-start
  8.0 0.0 copy-start.2
  8.0 0.0 reduce-scatter.5.cloned.1.call-start
  8.1 0.9 reshape.62
  8.9 0.1 add_bitcast_fusion
  9.0 0.8 dynamic_slice.12
  9.8 0.2 add_dynamic-update-slice_fusion
  9.9 42.1 %all-reduce = s32[3072]{0:T(1024)S(1)} all-reduce(s32[3072]{0:T(1024)S(1)} %add_dynamic-update-slice_fusion), channel_id=2, replica_groups=mesh['query'=8,'item'=4] {'query','item'}, use_global_device_ids=true, to_apply=%add | all-reduce | flops 3072 | bytes 24576
  52.1 0.1 reshape.63
  52.1 0.1 slice.22
  52.2 0.1 eq.16
  52.3 0.1 copy.26
  52.4 0.1 copy.20
  52.5 31.0 %all_gather.21 = bf16[512,256]{1,0:T(8,128)(2,1)S(1)} all-gather(bf16[64,256]{1,0:T(8,128)(2,1)} %param.6), channel_id=1, replica_groups=mesh['query'=8,'item'=4] {'query'}, dimensions={0}, use_global_device_ids=true | all-gather | bytes 294912 | tf_op jit(solution)/shard_map/all_gather | solution.py:18
  83.5 0.3 broadcast_in_dim.19
  83.9 0.0 copy-start.3
  83.9 0.3 copy.30
  84.2 0.6 copy.21
  84.8 0.0 copy-done
  84.8 0.0 copy-done.2
  84.8 0.4 fusion.11
  85.2 0.0 copy-done.3
  85.3 0.0 copy-start.1
  85.3 0.4 convolution_convert_fusion
  85.7 0.5 copy-done.1
  86.2 8.0 %all_gather.20 = bf16[1024,256]{1,0:T(8,128)(2,1)S(1)} all-gather(bf16[256,256]{1,0:T(8,128)(2,1)S(1)} %convolution_convert_fusion), channel_id=1, replica_groups=mesh['query'=8,'item'=4] {'item'}, dimensions={0}, use_global_device_ids=true | all-gather | bytes 655360 | tf_op jit(solution)/shard_map/all_gather | solution.py:34
  94.2 0.6 fusion.3
  94.8 0.8 select_reduce_fusion
  95.7 30.5 %all-gather.2 = f32[8,3,512]{2,1,0:T(4,128)S(1)} all-gather(f32[1,3,512]{2,1,0:T(4,128)S(1)} %maximum_bitcast_fusion), channel_id=3, replica_groups=mesh['query'=8,'item'=4] {'query'}, dimensions={0}, use_global_device_ids=true | all-gather | bytes 55296 | tf_op jit(solution)/shard_map/all_gather | solution.py:48
  126.2 0.1 fusion.24
  126.3 0.8 fusion.2
  127.1 1.4 convolution_multiply_fusion.1
  128.5 0.0 reduce-scatter.5.cloned.1.call-update
  128.5 0.0 all-reduce.4.cloned.1.call-start
  128.6 23.9 %reduce-scatter.5.cloned.1.call-done = f32[256,256]{1,0:T(8,128)} async-done(((f32[1024,256]{1,0:T(8,128)}), f32[256,256]{1,0:T(8,128)}) %reduce-scatter.5.cloned.1.call-update) | async-done | bytes 262160 | tf_op jit(solution)/shard_map/reduce_scatter | solution.py:58
  152.4 2.8 fusion.13
  155.2 3.4 %convolution_bitcast_fusion = f32[512,1024]{0,1:T(8,128)} fusion(bf16[1024,256]{1,0:T(8,128)(2,1)S(1)} %copy-done.3, f32[256,1024]{1,0:T(8,128)} %copy-done.1, bf16[1,256,512]{2,1,0:T(8,128)(2,1)S(1)} %copy-done.2, f32[256,256]{1,0:T(8,128)} %reduce-scatter.5.cloned.1.call-done), kind=kOutput, calls=%fused_computation.7 | convolution fusion | flops 405078016 | bytes 4194304 | tf_op jit(solution)/shard_map/id,ih->dh/dot_general | solution.py:67
  158.7 0.0 all-reduce.4.cloned.1.call-update
  158.7 0.0 reduce-scatter.3.cloned.1.call-start
  158.8 1.3 convolution_multiply_fusion.2
  160.0 0.0 reduce-scatter.3.cloned.1.call-update
  160.1 0.6 dynamic_slice.15
  160.6 136.9 %all-reduce.4.cloned.1.call-done = (f32[512,1024]{0,1:T(8,128)}, f32[1024,256]{1,0:T(8,128)}) async-done(((f32[512,1024]{0,1:T(8,128)}, f32[1024,256]{1,0:T(8,128)}), (f32[512,1024]{0,1:T(8,128)}, f32[1024,256]{1,0:T(8,128)})) %all-reduce.4.cloned.1.call-update) | async-done | bytes 3145744 | tf_op jit(solution)/shard_map/psum | solution.py:68
  297.6 1.8 broadcast_multiply_fusion
  299.4 1.8 copy.25
  301.2 2.3 broadcast_multiply_fusion.1
  303.5 0.0 reduce-scatter.3.cloned.1.call-done
  (8 shorter events, 0.1 us)
Async XLA Ops:
  8.0 76.8 %copy-start = (bf16[512,1024]{1,0:T(8,128)(2,1)S(1)}, bf16[512,1024]{1,0:T(8,128)(2,1)}, u32[]{:S(2)}) copy-start(bf16[512,1024]{1,0:T(8,128)(2,1)} %param.10) | copy-start | bytes 3145732
  8.0 76.8 %copy-start.2 = (bf16[1,256,512]{2,1,0:T(8,128)(2,1)S(1)}, bf16[1,256,512]{2,1,0:T(8,128)(2,1)}, u32[]{:S(2)}) copy-start(bf16[1,256,512]{2,1,0:T(8,128)(2,1)} %param.9) | copy-start | bytes 786436
  8.0 144.4 %reduce-scatter.5.cloned.1.call-start = ((), (), s32[]{:S(2)}) async-start(), calls=%async_computation.3 | async-start | bytes 1310720 | tf_op jit(solution)/shard_map/reduce_scatter | solution.py:58
  83.9 1.4 copy-start.3
  85.3 1.0 copy-start.1
  128.5 169.1 %all-reduce.4.cloned.1.call-start = ((), (), s32[]{:S(2)}) async-start(), calls=%async_computation.4 | async-start | bytes 6291456 | tf_op jit(solution)/shard_map/psum | solution.py:68
  158.7 144.8 %reduce-scatter.3.cloned.1.call-start = ((), (), s32[]{:S(2)}) async-start(), calls=%async_computation.2 | async-start | bytes 589824 | tf_op jit(solution)/shard_map/reduce_scatter | solution.py:62
Sparse Core Ops, SparseCore 0:
  128.6 23.7 reduce-scatter.4
  158.8 138.7 all-reduce.3
Sparse Core Ops, SparseCore 1:
  163.1 62.8 reduce-scatter.2
where the time goes:
time: 311 us
  waiting for transfers between devices  161 us (52%)
  blocking collectives  112 us (36%)
  between operations  15.7 us (5%)
  matrix products  10.3 us (3%)
  local copies, waits for them, and re-layouts  6.23 us (2%)
  other arithmetic  6.14 us (2%)
    psum x1, waiting for transfers between devices, on_device(): tower_sums = lax.psum((first_term, second_term), BOTH)  137 us
    unnamed x1, blocking collectives  42.1 us
    all_gather x1, blocking collectives, on_device(): queries = lax.all_gather(query_emb, 'query', axis=0, tiled=True)  31 us
    all_gather x1, blocking collectives, on_device(): stats = lax.all_gather(jnp.stack([top, total, positive]), 'query', axis=0)  30.5 us
    reduce_scatter x1, waiting for transfers between devices, on_device(): lax.psum_scatter(e_part, 'item', scatter_dimension=0, tiled=True)  23.9 us
    all_gather x1, blocking collectives, on_device(): items = lax.all_gather(own_emb, 'item', axis=0, tiled=True)  8.01 us
  transfers between devices with their start and end apart: 3, of which 2 were waited for; matrix products, arithmetic and copies ran while one was open for 3% of the time, Pallas kernels for 0%

commit v1 on v0

--- a/solution.py
+++ b/solution.py
@@ -65,7 +65,7 @@
     gate_sig = jax.nn.sigmoid(pre_act)
     pre_grad = (hid_grad * gate_sig * (1.0 + pre_act * (1.0 - gate_sig))).astype(jnp.bfloat16)
     first_term = jnp.einsum("id,ih->dh", tokens, pre_grad, preferred_element_type=jnp.float32)
-    tower_sums = lax.psum((first_term, second_term), BOTH)
+    tower_sums = lax.psum(lax.psum((first_term, second_term), "item"), "query")
     grad_scale = 1.0 / math.sqrt(block_rows * query_count * item_count)
     return (loss, query_grad, tower_sums[0] * grad_scale, tower_sums[1] * grad_scale)
 

time: 311 us -> 432 us (1.39)
  waiting for transfers between devices: 161 us -> 283 us
    psum x1 -> x2, waiting for transfers between devices: 137 us -> 200 us  [on_device(): tower_sums = lax.psum(lax.psum((first_term, second_term), 'item'), 'query')]
    reduce_scatter x1, waiting for transfers between devices: 0.01 us -> 58.7 us  [on_device(): lax.psum_scatter(q_part, 'query', scatter_dimension=0, tiled=True)]
  transfers between devices with their start and end apart: 3 -> 4, of which waited for: 2 -> 4; matrix products, arithmetic and copies ran while one was open for 3% -> 2% of each run, Pallas kernels for 0% -> 0%
where the time goes in v1:
time: 432 us
  waiting for transfers between devices  283 us (66%)
  blocking collectives  112 us (26%)
  between operations  13.9 us (3%)
  matrix products  10.3 us (2%)
  local copies, waits for them, and re-layouts  6.24 us (1%)
  other arithmetic  6.14 us (1%)
    psum x2, waiting for transfers between devices, on_device(): tower_sums = lax.psum(lax.psum((first_term, second_term), 'item'), 'query')  200 us
    reduce_scatter x1, waiting for transfers between devices, on_device(): lax.psum_scatter(q_part, 'query', scatter_dimension=0, tiled=True)  58.7 us
    unnamed x1, blocking collectives  42.1 us
    all_gather x1, blocking collectives, on_device(): queries = lax.all_gather(query_emb, 'query', axis=0, tiled=True)  31 us
    all_gather x1, blocking collectives, on_device(): stats = lax.all_gather(jnp.stack([top, total, positive]), 'query', axis=0)  30.5 us
    reduce_scatter x1, waiting for transfers between devices, on_device(): lax.psum_scatter(e_part, 'item', scatter_dimension=0, tiled=True)  23.9 us
  transfers between devices with their start and end apart: 4, of which 4 were waited for; matrix products, arithmetic and copies ran while one was open for 2% of the time, Pallas kernels for 0%

profile of v1, /device:TPU:0, one launch (start us, length us, event | category | flops | bytes accessed | tf_op | source)
XLA Modules:
  0.0 431.5 jit_solution(1064269458471591446)
XLA Ops:
  7.2 0.0 copy-start
  7.2 0.0 copy-start.2
  7.2 0.0 reduce-scatter.5.cloned.1.call-start
  7.3 0.9 reshape.62
  8.1 0.1 add_bitcast_fusion
  8.2 0.8 dynamic_slice.12
  8.9 0.2 add_dynamic-update-slice_fusion
  9.1 42.1 %all-reduce = s32[3072]{0:T(1024)S(1)} all-reduce(s32[3072]{0:T(1024)S(1)} %add_dynamic-update-slice_fusion), channel_id=2, replica_groups=mesh['query'=8,'item'=4] {'query','item'}, use_global_device_ids=true, to_apply=%add | all-reduce | flops 3072 | bytes 24576
  51.2 0.1 reshape.63
  51.3 0.1 slice.22
  51.4 0.1 eq.16
  51.5 0.1 copy.26
  51.6 0.1 copy.20
  51.7 31.0 %all_gather.21 = bf16[512,256]{1,0:T(8,128)(2,1)S(1)} all-gather(bf16[64,256]{1,0:T(8,128)(2,1)} %param.6), channel_id=1, replica_groups=mesh['query'=8,'item'=4] {'query'}, dimensions={0}, use_global_device_ids=true | all-gather | bytes 294912 | tf_op jit(solution)/shard_map/all_gather | solution.py:18
  82.7 0.3 broadcast_in_dim.19
  83.0 0.0 copy-start.3
  83.0 0.3 copy.30
  83.3 0.6 copy.21
  84.0 0.4 fusion.11
  84.4 0.0 copy-done.3
  84.4 0.0 copy-start.1
  84.4 0.4 convolution_convert_fusion
  84.8 0.5 copy-done.1
  85.4 8.0 %all_gather.20 = bf16[1024,256]{1,0:T(8,128)(2,1)S(1)} all-gather(bf16[256,256]{1,0:T(8,128)(2,1)S(1)} %convolution_convert_fusion), channel_id=1, replica_groups=mesh['query'=8,'item'=4] {'item'}, dimensions={0}, use_global_device_ids=true | all-gather | bytes 655360 | tf_op jit(solution)/shard_map/all_gather | solution.py:34
  93.4 0.6 fusion.3
  93.9 0.8 select_reduce_fusion
  94.8 30.5 %all-gather.2 = f32[8,3,512]{2,1,0:T(4,128)S(1)} all-gather(f32[1,3,512]{2,1,0:T(4,128)S(1)} %maximum_bitcast_fusion), channel_id=3, replica_groups=mesh['query'=8,'item'=4] {'query'}, dimensions={0}, use_global_device_ids=true | all-gather | bytes 55296 | tf_op jit(solution)/shard_map/all_gather | solution.py:48
  125.3 0.1 fusion.24
  125.4 0.8 fusion.2
  126.2 1.4 convolution_multiply_fusion.1
  127.6 0.0 reduce-scatter.5.cloned.1.call-update
  127.7 0.0 all-reduce.8.cloned.1.call-start
  127.7 23.9 %reduce-scatter.5.cloned.1.call-done = f32[256,256]{1,0:T(8,128)} async-done(((f32[1024,256]{1,0:T(8,128)}), f32[256,256]{1,0:T(8,128)}) %reduce-scatter.5.cloned.1.call-update) | async-done | bytes 262160 | tf_op jit(solution)/shard_map/reduce_scatter | solution.py:58
  151.6 2.8 fusion.13
  154.4 3.5 convolution_bitcast_fusion
  157.8 0.0 all-reduce.8.cloned.1.call-update
  157.8 0.0 all-reduce.6.cloned.1.call-start
  157.9 68.7 %all-reduce.8.cloned.1.call-done = (f32[512,1024]{0,1:T(8,128)}, f32[1024,256]{1,0:T(8,128)}) async-done(((f32[512,1024]{0,1:T(8,128)}, f32[1024,256]{1,0:T(8,128)}), (f32[512,1024]{0,1:T(8,128)}, f32[1024,256]{1,0:T(8,128)})) %all-reduce.8.cloned.1.call-update) | async-done | bytes 3145744 | tf_op jit(solution)/shard_map/psum | solution.py:68
  226.6 0.0 all-reduce.6.cloned.1.call-update
  226.7 0.0 reduce-scatter.3.cloned.1.call-start
  226.7 1.3 convolution_multiply_fusion.2
  228.0 0.0 reduce-scatter.3.cloned.1.call-update
  228.0 0.6 dynamic_slice.15
  228.6 131.7 %all-reduce.6.cloned.1.call-done = (f32[512,1024]{0,1:T(8,128)}, f32[1024,256]{1,0:T(8,128)}) async-done(((f32[512,1024]{0,1:T(8,128)}, f32[1024,256]{1,0:T(8,128)}), (f32[512,1024]{0,1:T(8,128)}, f32[1024,256]{1,0:T(8,128)})) %all-reduce.6.cloned.1.call-update) | async-done | bytes 3145744 | tf_op jit(solution)/shard_map/psum | solution.py:68
  360.3 1.8 broadcast_multiply_fusion
  362.1 1.8 copy.25
  364.0 2.3 broadcast_multiply_fusion.1
  366.2 58.7 %reduce-scatter.3.cloned.1.call-done = f32[64,256]{1,0:T(8,128)} async-done(((f32[512,256]{1,0:T(8,128)}), f32[64,256]{1,0:T(8,128)}) %reduce-scatter.3.cloned.1.call-update) | async-done | bytes 65552 | tf_op jit(solution)/shard_map/reduce_scatter | solution.py:62
  (10 shorter events, 0.1 us)
Async XLA Ops:
  7.2 76.8 %copy-start = (bf16[512,1024]{1,0:T(8,128)(2,1)S(1)}, bf16[512,1024]{1,0:T(8,128)(2,1)}, u32[]{:S(2)}) copy-start(bf16[512,1024]{1,0:T(8,128)(2,1)} %param.10) | copy-start | bytes 3145732
  7.2 76.8 %copy-start.2 = (bf16[1,256,512]{2,1,0:T(8,128)(2,1)S(1)}, bf16[1,256,512]{2,1,0:T(8,128)(2,1)}, u32[]{:S(2)}) copy-start(bf16[1,256,512]{2,1,0:T(8,128)(2,1)} %param.9) | copy-start | bytes 786436
  7.2 144.4 %reduce-scatter.5.cloned.1.call-start = ((), (), s32[]{:S(2)}) async-start(), calls=%async_computation.3 | async-start | bytes 1310720 | tf_op jit(solution)/shard_map/reduce_scatter | solution.py:58
  83.0 1.4 copy-start.3
  84.4 1.0 copy-start.1
  127.7 99.0 %all-reduce.8.cloned.1.call-start = ((), (), s32[]{:S(2)}) async-start(), calls=%async_computation.5 | async-start | bytes 6291456 | tf_op jit(solution)/shard_map/psum | solution.py:68
  157.8 202.4 %all-reduce.6.cloned.1.call-start = ((), (), s32[]{:S(2)}) async-start(), calls=%async_computation.4 | async-start | bytes 6291456 | tf_op jit(solution)/shard_map/psum | solution.py:68
  226.7 198.3 %reduce-scatter.3.cloned.1.call-start = ((), (), s32[]{:S(2)}) async-start(), calls=%async_computation.2 | async-start | bytes 589824 | tf_op jit(solution)/shard_map/reduce_scatter | solution.py:62
Sparse Core Ops, SparseCore 0:
  127.8 23.7 reduce-scatter.4
  158.0 68.6 all-reduce.7
  230.8 129.4 all-reduce.5
  364.1 60.8 reduce-scatter.2
